TPU v7x, 128 devices: a whole 4x4x4 slice. The times are simulated.
128 devices in a mesh: seq: 32 (over x, y, core), head: 4 (over z).
Axes of the slice: x: 4, y: 4, z: 4, core: 2. Of those that a mesh axis runs over, the one named last changes fastest.
Arguments:
- queries: bfloat16 [2, 8192, 20, 128], P(None, ('seq', 'head')), may hold values from -96 to 96
- grad_out: bfloat16 [2, 8192, 20, 128], P(None, ('seq', 'head')), may hold values from -6 to 6
- keys: bfloat16 [8192, 4, 128], P('seq', 'head'), may hold values from -6 to 6
- values: bfloat16 [8192, 4, 128], P('seq', 'head'), may hold values from -6 to 6
- doc_start: int32 [8192], replicated, may hold values from 0 to 8191, as said below
Outputs:
- query_grads: bfloat16 [2, 8192, 20, 128], P(None, ('seq', 'head'))
- key_grads: bfloat16 [8192, 4, 128], P('seq', 'head')
- value_grads: bfloat16 [8192, 4, 128], P('seq', 'head')
Inputs may be any that keep to these rules, and one draw needn't show every extreme that they name: doc_start[i] is the first position of token i's document, so doc_start[i] <= i; it is 0 for every token before position 4096, at most four documents begin at or after it, and the last token begins a document of its own.
All inputs are finite; a program needn't handle non-finite values.
Results may differ from a plain program's by a relative error of at most 0.005.
Values may be sent and summed in bfloat16 or wider, within the bound.
A program may use at most 128 MiB of HBM per device.

v0:
```python
import math

import jax
import jax.numpy as jnp
from jax import lax
from jax.sharding import PartitionSpec as P

NEG_START = -1e30


def block_length(key_count):
    return math.gcd(key_count, 1024)


def over_blocks(advance, carried, pieces):
    key_count = pieces[0].shape[0]
    block_rows = block_length(key_count)

    def one_block(block_index, inner):
        block_start = block_index * block_rows
        sliced = tuple(
            (
                lax.dynamic_slice_in_dim(piece_rows, block_start, block_rows, 0)
                for piece_rows in pieces
            )
        )
        return advance(inner, sliced, block_start)

    return lax.fori_loop(0, key_count // block_rows, one_block, carried)


def masked_scores(group, key_block, key_start, score_scale):
    query_rows, grad_rows, starts, positions = group
    key_pos = key_start + jnp.arange(key_block.shape[0], dtype=jnp.int32)
    allowed = (key_pos[None, :] >= starts[:, None]) & (key_pos[None, :] <= positions[:, None])
    scores = (
        jnp.einsum("lrkgd,nkd->lkgrn", query_rows, key_block, preferred_element_type=jnp.float32)
        * score_scale
    )
    return jnp.where(allowed, scores, -jnp.inf)


def stats_update(group, carried, key_block, value_block, key_start, score_scale):

    def stats_compute(inner):
        row_max, row_sum, weighted = inner
        scores = masked_scores(group, key_block, key_start, score_scale)
        new_max = jnp.maximum(row_max, jnp.max(scores, axis=-1))
        raw_weights = jnp.exp(scores - new_max[..., None])
        grad_probs = jnp.einsum(
            "lrkgd,nkd->lkgrn", group[1], value_block, preferred_element_type=jnp.float32
        )
        rescale = jnp.exp(row_max - new_max)
        return (
            new_max,
            row_sum * rescale + jnp.sum(raw_weights, axis=-1),
            weighted * rescale + jnp.sum(raw_weights * grad_probs, axis=-1),
        )

    return lax.cond(key_start > jnp.max(group[3]), lambda inner: inner, stats_compute, carried)


def grads_update(group, row_stats, carried, key_block, value_block, key_start, score_scale):
    log_norm, row_delta = row_stats

    def grads_compute(inner):
        query_acc, key_buffer, value_buffer = inner
        scores = masked_scores(group, key_block, key_start, score_scale)
        prob_rows = jnp.exp(scores - log_norm[..., None])
        grad_probs = jnp.einsum(
            "lrkgd,nkd->lkgrn", group[1], value_block, preferred_element_type=jnp.float32
        )
        grad_scores = prob_rows * (grad_probs - row_delta[..., None])
        grad_low = grad_scores.astype(jnp.bfloat16)
        prob_low = prob_rows.astype(jnp.bfloat16)
        query_acc = query_acc + jnp.einsum(
            "lkgrn,nkd->lrkgd", grad_low, key_block, preferred_element_type=jnp.float32
        )
        key_part = jnp.einsum(
            "lkgrn,lrkgd->nkd", grad_low, group[0], preferred_element_type=jnp.float32
        )
        value_part = jnp.einsum(
            "lkgrn,lrkgd->nkd", prob_low, group[1], preferred_element_type=jnp.float32
        )
        block_rows = key_block.shape[0]
        key_buffer = lax.dynamic_update_slice_in_dim(
            key_buffer,
            lax.dynamic_slice_in_dim(key_buffer, key_start, block_rows, 0) + key_part,
            key_start,
            0,
        )
        value_buffer = lax.dynamic_update_slice_in_dim(
            value_buffer,
            lax.dynamic_slice_in_dim(value_buffer, key_start, block_rows, 0) + value_part,
            key_start,
            0,
        )
        return (query_acc, key_buffer, value_buffer)

    return lax.cond(key_start > jnp.max(group[3]), lambda inner: inner, grads_compute, carried)


def layer_pass(groups, keys, values, score_scale, total_rows):
    stat_init = []
    for group in groups:
        layer_count, row_count, key_heads, group_size, head_width = group[0].shape
        stat_shape = (layer_count, key_heads, group_size, row_count)
        stat_init.append(
            (
                jnp.full(stat_shape, NEG_START, jnp.float32),
                jnp.zeros(stat_shape, jnp.float32),
                jnp.zeros(stat_shape, jnp.float32),
            )
        )

    def advance(inner, sliced, key_start):
        return tuple(
            (
                stats_update(group, member, sliced[0], sliced[1], key_start, score_scale)
                for group, member in zip(groups, inner)
            )
        )

    gathered_stats = over_blocks(
        advance,
        tuple(stat_init),
        (
            lax.all_gather(keys, "seq", axis=0, tiled=True),
            lax.all_gather(values, "seq", axis=0, tiled=True),
        ),
    )
    row_stats = tuple(
        ((member[0] + jnp.log(member[1]), member[2] / member[1]) for member in gathered_stats)
    )
    buffer_shape = (total_rows, keys.shape[1], keys.shape[2])
    grad_init = (
        tuple((jnp.zeros(group[0].shape, jnp.float32) for group in groups)),
        jnp.zeros(buffer_shape, jnp.float32),
        jnp.zeros(buffer_shape, jnp.float32),
    )

    def advance(inner, sliced, key_start):
        query_accs, key_buffer, value_buffer = inner
        updated = []
        for group, stats_pair, query_acc in zip(groups, row_stats, query_accs):
            query_acc, key_buffer, value_buffer = grads_update(
                group,
                stats_pair,
                (query_acc, key_buffer, value_buffer),
                sliced[0],
                sliced[1],
                key_start,
                score_scale,
            )
            updated.append(query_acc)
        return (tuple(updated), key_buffer, value_buffer)

    query_accs, key_buffer, value_buffer = over_blocks(
        advance,
        grad_init,
        (
            lax.all_gather(keys, "seq", axis=0, tiled=True),
            lax.all_gather(values, "seq", axis=0, tiled=True),
        ),
    )
    key_own, value_own = (
        lax.psum_scatter(key_buffer, "seq", scatter_dimension=0, tiled=True),
        lax.psum_scatter(value_buffer, "seq", scatter_dimension=0, tiled=True),
    )
    return (query_accs, key_own, value_own)


def per_device(queries, grad_out, keys, values, doc_start):
    layer_count = queries.shape[0]
    head_width = queries.shape[3]
    key_heads = keys.shape[1]
    score_scale = 1.0 / math.sqrt(head_width)
    regrouped, regrads = (
        lax.all_to_all(queries, "head", split_axis=2, concat_axis=1, tiled=True),
        lax.all_to_all(grad_out, "head", split_axis=2, concat_axis=1, tiled=True),
    )
    row_count = regrouped.shape[1]
    local_heads = regrouped.shape[2]
    group_size = local_heads // key_heads
    five_shape = (layer_count, row_count, key_heads, group_size, head_width)
    query_rows = regrouped.reshape(five_shape)
    grad_rows = regrads.reshape(five_shape)
    seq_index = lax.axis_index("seq")
    seq_count = lax.axis_size("seq")
    total_rows = row_count * seq_count
    offsets = jnp.arange(row_count, dtype=jnp.int32)
    own_pos = seq_index * row_count + offsets
    own_start = lax.dynamic_slice_in_dim(doc_start, seq_index * row_count, row_count, 0)
    groups = ((query_rows, grad_rows, own_start, own_pos),)
    collected = []
    for layer_index in range(layer_count):
        sliced = tuple(
            (
                (
                    group[0][layer_index : layer_index + 1],
                    group[1][layer_index : layer_index + 1],
                    group[2],
                    group[3],
                )
                for group in groups
            )
        )
        accs, key_own, value_own = layer_pass(sliced, keys, values, score_scale, total_rows)
        collected.append(accs)
        if layer_index == 0:
            key_total, value_total = (key_own, value_own)
        else:
            key_total, value_total = (key_total + key_own, value_total + value_own)
    query_accs = tuple(
        (
            jnp.concatenate([accs[member] for accs in collected], axis=0)
            for member in range(len(groups))
        )
    )
    query_low = tuple(((acc * score_scale).astype(jnp.bfloat16) for acc in query_accs))
    query_final = query_low[0]
    query_final = query_final.reshape(layer_count, row_count, local_heads, head_width)
    query_grads = lax.all_to_all(query_final, "head", split_axis=1, concat_axis=2, tiled=True)
    key_grads = (key_total * score_scale).astype(jnp.bfloat16)
    value_grads = value_total.astype(jnp.bfloat16)
    return (query_grads, key_grads, value_grads)


def solution(mesh):
    in_specs = (
        P(None, ("seq", "head"), None, None),
        P(None, ("seq", "head"), None, None),
        P("seq", "head", None),
        P("seq", "head", None),
        P(),
    )
    out_specs = (
        P(None, ("seq", "head"), None, None),
        P("seq", "head", None),
        P("seq", "head", None),
    )
    return jax.shard_map(
        per_device, mesh=mesh, in_specs=in_specs, out_specs=out_specs, check_vma=False
    )
```

profile of v0, /device:TPU:1, one launch (start us, length us, event | category | flops | bytes accessed | tf_op | source)
XLA Modules:
  0.0 596.9 jit_solution(12327094851569278671)
XLA Ops:
  7.2 0.7 all-gather.3.cloned.1.call-update
  7.9 0.7 all-gather.5.cloned.1.call-update
  8.6 2.0 copy.50
  10.6 5.8 all-to-all-start
  16.5 2.0 copy.52
  18.5 8.0 %all-to-all-done = bf16[2,64,20,128]{3,1,0,2:T(8,128)(2,1)S(1)} async-done(((bf16[2,64,20,128]{3,1,0,2:T(8,128)(2,1)}), bf16[2,64,20,128]{3,1,0,2:T(8,128)(2,1)S(1)}, u32[]{:S(2)}, u32[]{:S(2)}) %all-to-all-start) | async-done | bytes 655392 | tf_op jit(solution)/shard_map/all_to_all | solution.py:179
  26.5 3.5 all-to-all-start.1
  30.6 0.8 dynamic_slice.139
  31.5 7.3 %all-to-all-done.1 = bf16[2,64,20,128]{3,1,0,2:T(8,128)(2,1)S(1)} async-done(((bf16[2,64,20,128]{3,1,0,2:T(8,128)(2,1)}), bf16[2,64,20,128]{3,1,0,2:T(8,128)(2,1)S(1)}, u32[]{:S(2)}, u32[]{:S(2)}) %all-to-all-start.1) | async-done | bytes 655392 | tf_op jit(solution)/shard_map/all_to_all | solution.py:180
  38.9 18.3 %all-gather.3.cloned.1.call-done = bf16[8192,1,128]{2,0,1:T(8,128)(2,1)} async-done(((bf16[256,1,128]{2,0,1:T(8,128)(2,1)}), bf16[8192,1,128]{2,0,1:T(8,128)(2,1)}) %all-gather.3.cloned.1.call-update) | async-done | bytes 2097168 | tf_op jit(solution)/shard_map/all_gather | solution.py:162
  57.3 45.1 %all-gather.5.cloned.1.call-done = bf16[8192,1,128]{2,0,1:T(8,128)(2,1)} async-done(((bf16[256,1,128]{2,0,1:T(8,128)(2,1)}), bf16[8192,1,128]{2,0,1:T(8,128)(2,1)}) %all-gather.5.cloned.1.call-update) | async-done | bytes 2097168 | tf_op jit(solution)/shard_map/all_gather | solution.py:163
  102.4 10.8 %while.76 = (s32[]{:T(128)}, f32[1,1,5,256]{3,2,1,0:T(8,128)S(1)}, f32[1,1,5,256]{3,2,1,0:T(8,128)S(1)}, f32[1,1,5,256]{3,2,1,0:T(8,128)S(1)}, s32[]{:T(128)}, /...) while((s32[]{:T(128)}, f32[1,1,5,256]{3,2,1,0:T(8,128)S(1)}, ...), condition=%wide.region_7.8_spmd.clone, body=%wide.region_1.7_spmd.clone.sunk | while | flops 687608832 | bytes 18062672 | solution.py:29
  102.9 5.9 conditional.12
  103.3 1.9 fusion.10
  105.2 2.5 fusion.8
  107.7 1.1 fusion.9
  113.3 10.8 %while.78 = (s32[]{:T(128)}, f32[1,1,5,256]{3,2,1,0:T(8,128)S(1)}, f32[1,1,5,256]{3,2,1,0:T(8,128)S(1)}, f32[1,1,5,256]{3,2,1,0:T(8,128)S(1)}, s32[]{:T(128)}, /...) while((s32[]{:T(128)}, f32[1,1,5,256]{3,2,1,0:T(8,128)S(1)}, ...), condition=%wide.region_18.19_spmd.clone, body=%wide.region_12.18_spmd.clone.sunk | while | flops 687608832 | bytes 18062672 | solution.py:29
  113.8 5.9 conditional.14
  114.2 1.9 fusion.60
  116.1 2.5 fusion.58
  118.6 1.1 fusion.59
  124.2 2.2 broadcast.98.clone.1
  126.4 2.2 broadcast.98.clone
  128.6 16.9 %while.79 = (s32[]{:T(128)}, f32[1,256,1,5,128]{1,4,3,0,2:T(8,128)S(1)}, f32[8192,1,128]{2,0,1:T(8,128)}, f32[8192,1,128]{2,0,1:T(8,128)}, s32[]{:T(128)}, /*ind...) while((s32[]{:T(128)}, ...), condition=%wide.region_22.23_spmd.clone, body=%wide.region_19.22_spmd.clone.sunk | while | flops 1692042496 | bytes 29913476 | solution.py:29
  129.2 12.2 %conditional.15 = ((f32[1,256,1,5,128]{1,4,3,0,2:T(8,128)S(1)}, f32[8192,1,128]{2,0,1:T(8,128)}, f32[8192,1,128]{2,0,1:T(8,128)})) conditional(s32[]{:T(128)} %convert_element_type.110, (s32[]{:T(128)}, bf16[8192,1,128]{2,0,1:T(8,128)(2,1)}, s32[256]{0:T(256)S(1)}, s32[]{:T(128)}, bf16[1,256,1,5,128]{4,1,3,2,0:T(8,128)(2,1)S(1)}, ...), branch_computations={%region_20.0_spmd, %region_21.21_spmd} | conditional | flops 1692042496 | bytes 29912158 | solution.py:100
  129.5 1.8 fusion.95
  131.3 2.6 fusion.76
  133.9 3.2 fusion.89
  137.0 1.5 fusion.85
  138.6 2.7 fusion.84
  145.6 2.2 broadcast.98.clone.2
  147.8 2.2 broadcast.98.clone.3
  150.1 16.9 %while.77 = (s32[]{:T(128)}, f32[1,256,1,5,128]{1,4,3,0,2:T(8,128)S(1)}, f32[8192,1,128]{2,0,1:T(8,128)}, f32[8192,1,128]{2,0,1:T(8,128)}, s32[]{:T(128)}, /*ind...) while((s32[]{:T(128)}, ...), condition=%wide.region_11.0_spmd.clone, body=%wide.region_8.11_spmd.clone.sunk | while | flops 1692042496 | bytes 29913476 | solution.py:29
  150.6 12.2 %conditional.13 = ((f32[1,256,1,5,128]{1,4,3,0,2:T(8,128)S(1)}, f32[8192,1,128]{2,0,1:T(8,128)}, f32[8192,1,128]{2,0,1:T(8,128)})) conditional(s32[]{:T(128)} %convert_element_type.108, (s32[]{:T(128)}, bf16[8192,1,128]{2,0,1:T(8,128)(2,1)}, s32[256]{0:T(256)S(1)}, s32[]{:T(128)}, bf16[1,256,1,5,128]{4,1,3,2,0:T(8,128)(2,1)S(1)}, ...), branch_computations={%region_9.9_spmd, %region_10.10_spmd} | conditional | flops 1692042496 | bytes 29912158 | solution.py:100
  151.0 1.8 fusion.45
  152.8 2.6 fusion.26
  155.4 3.2 fusion.39
  158.6 1.6 fusion.35
  160.1 2.7 fusion.34
  167.0 5.8 add.283
  173.1 5.9 add.282
  180.0 1.4 fusion.108
  181.4 14.3 %all_to_all.48 = bf16[2,256,5,128]{3,0,2,1:T(2,128)(2,1)S(1)} all-to-all(bf16[2,256,5,128]{3,0,2,1:T(2,128)(2,1)S(1)} %fusion.108), channel_id=1, replica_groups=mesh['seq'=32,'head'=4] {'head'}, dimensions={1} | all-to-all | bytes 1310720 | tf_op jit(solution)/shard_map/all_to_all | solution.py:223
  195.9 0.9 copy.59
  196.7 307.0 %reduce-scatter.5.cloned.1.call-done = f32[256,1,128]{2,0,1:T(8,128)} async-done(((f32[8192,1,128]{2,0,1:T(8,128)}), f32[256,1,128]{2,0,1:T(8,128)}) %reduce-scatter.5.cloned.1.call-update) | async-done | bytes 131088 | tf_op jit(solution)/shard_map/reduce_scatter | solution.py:168
  503.7 1.5 convert_element_type.70
  505.3 83.6 %reduce-scatter.3.cloned.1.call-done = f32[256,1,128]{2,0,1:T(8,128)} async-done(((f32[8192,1,128]{2,0,1:T(8,128)}), f32[256,1,128]{2,0,1:T(8,128)}) %reduce-scatter.3.cloned.1.call-update) | async-done | bytes 131088 | tf_op jit(solution)/shard_map/reduce_scatter | solution.py:167
  588.8 1.5 multiply_convert_fusion
  (132 shorter events, 4.4 us)
Async XLA Ops:
  7.2 50.1 %all-gather.3.cloned.1.call-start = ((), (), s32[]{:S(2)}) async-start(), calls=%async_computation.5 | async-start | bytes 2162688 | tf_op jit(solution)/shard_map/all_gather | solution.py:162
  7.9 94.5 %all-gather.5.cloned.1.call-start = ((), (), s32[]{:S(2)}) async-start(), calls=%async_computation.6 | async-start | bytes 2162688 | tf_op jit(solution)/shard_map/all_gather | solution.py:163
  10.6 15.9 %all-to-all-start = ((bf16[2,64,20,128]{3,1,0,2:T(8,128)(2,1)}), bf16[2,64,20,128]{3,1,0,2:T(8,128)(2,1)S(1)}, u32[]{:S(2)}, u32[]{:S(2)}) async-start(bf16[2,64,20,128]{3,1,0,2:T(8,128)(2,1)} %copy.50), calls=%async_computation | async-start | bytes 1310720 | tf_op jit(solution)/shard_map/all_to_all | solution.py:179
  26.5 12.3 %all-to-all-start.1 = ((bf16[2,64,20,128]{3,1,0,2:T(8,128)(2,1)}), bf16[2,64,20,128]{3,1,0,2:T(8,128)(2,1)S(1)}, u32[]{:S(2)}, u32[]{:S(2)}) async-start(bf16[2,64,20,128]{3,1,0,2:T(8,128)(2,1)} %copy.52), calls=%async_computation.1 | async-start | bytes 1310720 | tf_op jit(solution)/shard_map/all_to_all | solution.py:180
  30.0 473.7 %reduce-scatter.5.cloned.1.call-start = ((), (), s32[]{:S(2)}) async-start(), calls=%async_computation.8 | async-start | bytes 4325376 | tf_op jit(solution)/shard_map/reduce_scatter | solution.py:168
  172.9 416.0 %reduce-scatter.3.cloned.1.call-start = ((), (), s32[]{:S(2)}) async-start(), calls=%async_computation.7 | async-start | bytes 4325376 | tf_op jit(solution)/shard_map/reduce_scatter | solution.py:167
Sparse Core Ops, SparseCore 0:
  10.2 47.0 all-gather.2
  59.6 42.7 all-gather.4
  173.0 330.6 reduce-scatter.4
  507.2 81.5 reduce-scatter.2
where the time goes:
time: 603 us; the launch traced here: 597 us
  waiting for transfers between devices  471 us (78%)
  matrix products  32.5 us (5%)
  other arithmetic  20.2 us (3%)
  loops' own time  19.6 us (3%)
  local copies, waits for them, and re-layouts  16 us (3%)
  blocking collectives  14.3 us (2%)
  between operations  13.9 us (2%)
  starting transfers between devices  9.71 us (2%)
    reduce_scatter x1, waiting for transfers between devices, layer_pass(): lax.psum_scatter(value_buffer, 'seq', scatter_dimension=0, tiled=True)  307 us
    reduce_scatter x1, waiting for transfers between devices, layer_pass(): lax.psum_scatter(key_buffer, 'seq', scatter_dimension=0, tiled=True)  83.6 us
    all_gather x1, waiting for transfers between devices, layer_pass(): lax.all_gather(values, 'seq', axis=0, tiled=True)  45.1 us
    another operation x4, loops' own time, over_blocks(): return lax.fori_loop(0, key_count // block_rows, one_block, carried)  18.5 us
    all_gather x1, waiting for transfers between devices, layer_pass(): lax.all_gather(keys, 'seq', axis=0, tiled=True)  18.3 us
    all_to_all x1, blocking collectives, per_device(): lax.all_to_all(query_final, 'head', split_axis=1, concat_axis=2, tiled=True)  14.3 us
  transfers between devices with their start and end apart: 6, of which 6 were waited for; matrix products, arithmetic and copies ran while one was open for 3% of the time, Pallas kernels for 0%

commit v1 on v0

v1 whole, which is shorter than its diff:
```python
import functools
import math

import jax
import jax.numpy as jnp
from jax import lax
from jax.experimental import pallas as pl
from jax.experimental.pallas import tpu as pltpu
from jax.sharding import PartitionSpec as P

NEG = -1e30
ROUNDS = 10
BK = 1024
MESH = pl.DeviceIdType.MESH
NT = (((1,), (1,)), ((), ()))
TN = (((0,), (0,)), ((), ()))
ANY = pl.BlockSpec(memory_space=pl.ANY)
VM = pl.BlockSpec(memory_space=pltpu.VMEM)


def coords():
    s = lax.axis_index("seq")
    z = lax.axis_index("head")
    c = lax.rem(s, 2)
    y = lax.rem(s // 2, 4)
    x = s // 8
    return s, z, x, y, c


def seq_of(x, y, c):
    return (x * 4 + y) * 2 + c


def wrap(v):
    return lax.rem(v + 4, 4)


def unit_dest(n):
    r = n // 32
    p = lax.rem(n, 32)
    return r, jnp.where(lax.rem(r, 2) == 0, p, 31 - p)


def unit_at(r, s):
    return 32 * r + jnp.where(lax.rem(r, 2) == 0, s, 31 - s)


def at_dev(s, z):
    return {"seq": s, "head": z}


def gather_kernel(qh, gh, k, v, qbuf, gbuf, kfull, vfull, qsend, gsend, qrecv, grecv, ksend, vsend, krecv, vrecv, kpart, vpart, lsem):
    s, z, x, y, c = coords()
    half = lax.rem(z, 2)
    blk = 2 * s + z // 2
    dests = []
    for h in range(5):
        r, ds = unit_dest(5 * blk + h)
        for g in range(4):
            dests.append((h, g, r, ds))
    sources = []
    for r in range(ROUNDS):
        b = unit_at(r, s) // 5
        for hf in range(2):
            sources.append((b // 2, 2 * lax.rem(b, 2) + hf))

    barrier = pltpu.get_barrier_semaphore()
    selfs = jnp.int32(0)
    for ss, sz in sources:
        mine = jnp.logical_and(ss == s, sz == z)

        @pl.when(jnp.logical_not(mine))
        def _():
            pl.semaphore_signal(barrier, inc=1, device_id=at_dev(ss, sz), device_id_type=MESH)

        selfs = selfs + mine.astype(jnp.int32)
    ring = [(1, 0), (-1, 0), (0, 1), (0, -1)]
    for dx, dy in ring:
        pl.semaphore_signal(barrier, inc=1, device_id=at_dev(seq_of(wrap(x + dx), wrap(y + dy), c), z), device_id_type=MESH)
    pl.semaphore_signal(barrier, inc=1, device_id=at_dev(seq_of(x, y, 1 - c), z), device_id_type=MESH)
    pl.semaphore_wait(barrier, 25 - selfs)

    own = [
        pltpu.make_async_copy(k, kfull.at[s], lsem.at[0]),
        pltpu.make_async_copy(v, vfull.at[s], lsem.at[1]),
    ]
    for d in own:
        d.start()

    order = [(0, 0), (-1, 0), (1, 0), (0, -1), (0, 1), (2, 0), (-1, -1), (-1, 1), (1, -1), (1, 1), (2, -1), (2, 1), (0, 2), (-1, 2), (1, 2), (2, 2)]

    def mover(own_ref, full, send, recv, part, first_is_x):
        def dev(da, db, core):
            dx, dy = (da, db) if first_is_x else (db, da)
            return at_dev(seq_of(wrap(x + dx), wrap(y + dy), core), z)

        def slot(da, db):
            dx, dy = (da, db) if first_is_x else (db, da)
            return seq_of(wrap(x + dx), wrap(y + dy), c)

        sends = []
        state = [0]

        def recv_id(da, db, hi):
            da, db = (da + 1) % 4, (db + 1) % 4
            return (da * 4 + db) * 2 + hi

        def push(src, dst, target, rsem):
            d = pltpu.make_async_remote_copy(
                src_ref=src, dst_ref=dst, send_sem=send.at[state[0]], recv_sem=rsem, device_id=target, device_id_type=MESH
            )
            state[0] += 1
            d.start()
            sends.append(d)

        def await_(ref, sem):
            pltpu.make_async_copy(ref, ref, sem).wait()

        lo, hi = pl.ds(0, 128), pl.ds(128, 128)

        def step(da, db):
            sl = slot(da, db)
            dst = full.at[sl]
            src = own_ref if (da, db) == (0, 0) else dst
            if (da, db) != (0, 0):
                if da == 2 and db == 0 or db == 2:
                    await_(full.at[sl, lo], recv.at[recv_id(da, db, 0)])
                    await_(full.at[sl, hi], recv.at[recv_id(da, db, 1)])
                else:
                    await_(dst, recv.at[recv_id(da, db, 0)])
            if (da, db) == (0, 0):
                push(src, dst, dev(1, 0, c), recv.at[recv_id(-1, 0, 0)])
                push(src, dst, dev(-1, 0, c), recv.at[recv_id(1, 0, 0)])
            if db == 0:
                if da == -1:
                    push(full.at[sl, lo], full.at[sl, lo], dev(1, 0, c), recv.at[recv_id(2, 0, 0)])
                if da == 1:
                    push(full.at[sl, hi], full.at[sl, hi], dev(-1, 0, c), recv.at[recv_id(2, 0, 1)])
                push(src, dst, dev(0, 1, c), recv.at[recv_id(da, -1, 0)])
                push(src, dst, dev(0, -1, c), recv.at[recv_id(da, 1, 0)])
            if db == -1:
                push(full.at[sl, lo], full.at[sl, lo], dev(0, 1, c), recv.at[recv_id(da, 2, 0)])
            if db == 1:
                push(full.at[sl, hi], full.at[sl, hi], dev(0, -1, c), recv.at[recv_id(da, 2, 1)])
            push(src, dst, dev(0, 0, 1 - c), part.at[recv_id(da, db, 0)])

        def finish():
            for da, db in order:
                dx, dy = (da, db) if first_is_x else (db, da)
                sl = seq_of(wrap(x + dx), wrap(y + dy), 1 - c)
                await_(full.at[sl], part.at[recv_id(da, db, 0)])
            for d in sends:
                d.wait_send()

        return step, finish

    kstep, kfin = mover(k, kfull, ksend, krecv, kpart, True)
    vstep, vfin = mover(v, vfull, vsend, vrecv, vpart, False)

    kstep(0, 0)
    vstep(0, 0)

    moves = []
    for i, (h, g, r, ds) in enumerate(dests):
        mine = jnp.logical_and(ds == s, g == z)
        for srcs, buf, snd, rcv in ((qh, qbuf, qsend, qrecv), (gh, gbuf, gsend, grecv)):
            src = srcs.at[g * 5 + h]
            dst = buf.at[r, :, pl.ds(pl.multiple_of(half * 64, 64), 64), :]
            rem = pltpu.make_async_remote_copy(
                src_ref=src, dst_ref=dst, send_sem=snd.at[i], recv_sem=rcv, device_id=at_dev(ds, g), device_id_type=MESH
            )

            @pl.when(mine)
            def _():
                pltpu.make_async_copy(src, dst, rcv).start()

            @pl.when(jnp.logical_not(mine))
            def _():
                rem.start()

            moves.append((mine, rem))

    for da, db in order[1:]:
        kstep(da, db)
        vstep(da, db)
    kfin()
    vfin()
    pltpu.make_async_copy(qbuf, qbuf, qrecv).wait()
    pltpu.make_async_copy(gbuf, gbuf, grecv).wait()
    for mine, rem in moves:

        @pl.when(jnp.logical_not(mine))
        def _():
            rem.wait_send()

    for d in own:
        d.wait()


def gather(qh, gh, k, v):
    bf = jnp.bfloat16
    dma = pltpu.SemaphoreType.DMA
    return pl.pallas_call(
        gather_kernel,
        out_shape=(
            jax.ShapeDtypeStruct((ROUNDS, 2, 128, 128), bf),
            jax.ShapeDtypeStruct((ROUNDS, 2, 128, 128), bf),
            jax.ShapeDtypeStruct((32, 256, 128), bf),
            jax.ShapeDtypeStruct((32, 256, 128), bf),
        ),
        in_specs=[ANY] * 4,
        out_specs=(ANY,) * 4,
        scratch_shapes=[dma((20,)), dma((20,)), dma, dma, dma((40,)), dma((40,)), dma((32,)), dma((32,)), dma((32,)), dma((32,)), dma((2,))],
        compiler_params=pltpu.CompilerParams(collective_id=0, has_side_effects=True),
        name="gather_units",
    )(qh, gh, k, v)


def attn_kernel(doc_s, doc_v, q_ref, g_ref, k_ref, v_ref, dq_ref, dkv_ref, s_scr, p_scr, dk_acc, dv_acc):
    scale = 1.0 / math.sqrt(128)
    c = scale * math.log2(math.e)
    sidx = lax.axis_index("seq")
    dk_acc[...] = jnp.zeros_like(dk_acc)
    dv_acc[...] = jnp.zeros_like(dv_acc)

    def tile(r, _):
        first = (unit_at(r, sidx) // 5) * 128
        last = first + 127
        start_min = doc_s[first]
        start_max = doc_s[last]
        lo = start_min // BK
        hi = last // BK + 1
        fhi = jnp.minimum((first + 1) // BK, hi)
        flo = jnp.minimum(jnp.maximum(lo, (start_max + BK - 1) // BK), hi)
        fhi = jnp.maximum(fhi, flo)
        srow = doc_v[pl.ds(unit_at(r, sidx) // 5, 1), :]
        prow = first + lax.broadcasted_iota(jnp.int32, (1, 128), 1)
        srow = jnp.concatenate([srow, srow], axis=1)
        prow = jnp.concatenate([prow, prow], axis=1)
        q = q_ref[r]
        g = g_ref[r]

        def stats(masked, kb, carry):
            m, l, w = carry
            o = pl.multiple_of(kb * BK, BK)
            s = lax.dot_general(k_ref[pl.ds(o, BK), :], q, NT, preferred_element_type=jnp.float32)
            dp = lax.dot_general(v_ref[pl.ds(o, BK), :], g, NT, preferred_element_type=jnp.float32)
            if masked:
                kp = o + lax.broadcasted_iota(jnp.int32, (BK, 256), 0)
                s = jnp.where((kp >= srow) & (kp <= prow), s, NEG)
            s_scr[pl.ds(o, BK), :] = s
            p_scr[pl.ds(o, BK), :] = dp
            mn = jnp.maximum(m, jnp.max(s, axis=0, keepdims=True))
            a = jnp.exp2((m - mn) * c)
            e = jnp.exp2((s - mn) * c)
            l = l * a + jnp.sum(e, axis=0, keepdims=True)
            w = w * a + jnp.sum(e * dp, axis=0, keepdims=True)
            return mn, l, w

        zero = jnp.zeros((1, 256), jnp.float32)
        carry = (zero + NEG, zero, zero)
        carry = lax.fori_loop(lo, flo, functools.partial(stats, True), carry)
        carry = lax.fori_loop(flo, fhi, functools.partial(stats, False), carry)
        m, l, w = lax.fori_loop(fhi, hi, functools.partial(stats, True), carry)
        shift = m * c + jnp.log2(l)
        delta = w / l

        def grads(kb, acc):
            o = pl.multiple_of(kb * BK, BK)
            rows = pl.ds(o, BK)
            p = jnp.exp2(s_scr[rows, :] * c - shift)
            ds = p * (p_scr[rows, :] - delta)
            p16 = p.astype(jnp.bfloat16)
            d16 = ds.astype(jnp.bfloat16)
            dv_acc[rows, :] += jnp.dot(p16, g, preferred_element_type=jnp.float32)
            dk_acc[rows, :] += jnp.dot(d16, q, preferred_element_type=jnp.float32)
            return acc + lax.dot_general(d16, k_ref[rows, :], TN, preferred_element_type=jnp.float32)

        acc = lax.fori_loop(lo, hi, grads, jnp.zeros((256, 128), jnp.float32))
        dq_ref[r] = (acc * scale).astype(jnp.bfloat16)
        return 0

    lax.fori_loop(0, ROUNDS, tile, 0)
    dkv_ref[0] = (dk_acc[...] * scale).astype(jnp.bfloat16)
    dkv_ref[1] = dv_acc[...].astype(jnp.bfloat16)


def attn(doc, q, g, k, v):
    return pl.pallas_call(
        attn_kernel,
        out_shape=(
            jax.ShapeDtypeStruct((ROUNDS, 256, 128), jnp.bfloat16),
            jax.ShapeDtypeStruct((2, 8192, 128), jnp.bfloat16),
        ),
        in_specs=[pl.BlockSpec(memory_space=pltpu.SMEM), VM, VM, VM, VM, VM],
        out_specs=(VM, VM),
        scratch_shapes=[
            pltpu.VMEM((8192, 256), jnp.float32),
            pltpu.VMEM((8192, 256), jnp.float32),
            pltpu.VMEM((8192, 128), jnp.float32),
            pltpu.VMEM((8192, 128), jnp.float32),
        ],
        compiler_params=pltpu.CompilerParams(vmem_limit_bytes=62 << 20),
        name="attn_grads",
    )(doc, doc.reshape(64, 128), q, g, k, v)


def reduce_kernel(dq, dkv, dqo, kvo, own, part, send1, mid, rl_lo, rl_hi, from_l, from_r, send2, recv2, fin, dqsend, dqrecv, psend, precv, s1, r1, s2, r2, s3, r3, lsem):
    f32, bf = jnp.float32, jnp.bfloat16
    s, z, x, y, c = coords()
    partner = at_dev(seq_of(x, y, 1 - c), z)
    first_x = c == 0
    a0 = jnp.where(first_x, x, y)
    b0 = jnp.where(first_x, y, x)

    def dev(da, db):
        a, b = wrap(a0 + da), wrap(b0 + db)
        return at_dev(seq_of(jnp.where(first_x, a, b), jnp.where(first_x, b, a), c), z)

    units = []
    for r in range(ROUNDS):
        n = unit_at(r, s)
        b = n // 5
        for hf in range(2):
            units.append((r, hf, lax.rem(n, 5), b // 2, 2 * lax.rem(b, 2) + hf))

    barrier = pltpu.get_barrier_semaphore()
    blk = 2 * s + z // 2
    for h in range(5):
        _, ds = unit_dest(5 * blk + h)
        for g in range(4):
            @pl.when(jnp.logical_not(jnp.logical_and(ds == s, g == z)))
            def _():
                pl.semaphore_signal(barrier, inc=1, device_id=at_dev(ds, g), device_id_type=MESH)
    pl.semaphore_signal(barrier, inc=1, device_id=partner, device_id_type=MESH)
    for d in (1, -1):
        pl.semaphore_signal(barrier, inc=1, device_id=dev(d, 0), device_id_type=MESH)
    for d in (1, -1, 2):
        pl.semaphore_signal(barrier, inc=1, device_id=dev(0, d), device_id_type=MESH)
    selfs = jnp.int32(0)
    for r, hf, h, ss, sz in units:
        selfs = selfs + jnp.logical_and(ss == s, sz == z).astype(jnp.int32)
    pl.semaphore_wait(barrier, 26 - selfs)

    quarters = (2, 1, -1, 0)

    def blocks(ref, which, a, b):
        return ref.at[which, jnp.where(first_x, a, b), jnp.where(first_x, b, a)]

    exch = []
    loads = []
    for qi, d in enumerate(quarters):
        a = wrap(a0 + d)
        pa = wrap(b0 + d)
        for b in range(4):
            i = qi * 4 + b
            src = dkv.at[1 - c, jnp.where(first_x, b, pa), jnp.where(first_x, pa, b)]
            cp = pltpu.make_async_remote_copy(
                src_ref=src, dst_ref=part.at[qi, b], send_sem=psend.at[i], recv_sem=precv.at[i], device_id=partner, device_id_type=MESH
            )
            cp.start()
            exch.append(cp)
            ld = pltpu.make_async_copy(blocks(dkv, c, a, b), own.at[qi, b], lsem.at[i])
            ld.start()
            loads.append(ld)

    moves = []
    for i, (r, hf, h, ss, sz) in enumerate(units):
        mine = jnp.logical_and(ss == s, sz == z)
        src = dq.at[r, :, pl.ds(hf * 64, 64), :]
        dst = dqo.at[z * 5 + h]
        rem = pltpu.make_async_remote_copy(
            src_ref=src, dst_ref=dst, send_sem=dqsend.at[i], recv_sem=dqrecv, device_id=at_dev(ss, sz), device_id_type=MESH
        )

        @pl.when(mine)
        def _():
            pltpu.make_async_copy(src, dst, dqrecv).start()

        @pl.when(jnp.logical_not(mine))
        def _():
            rem.start()

        moves.append((mine, rem))

    def chip_sum(qi, b):
        i = qi * 4 + b
        exch[i].wait_recv()
        loads[i].wait()
        return own[qi, b].astype(f32) + part[qi, b].astype(f32)

    def push(src, dst, ss, rs, target):
        cp = pltpu.make_async_remote_copy(src_ref=src, dst_ref=dst, send_sem=ss, recv_sem=rs, device_id=target, device_id_type=MESH)
        cp.start()
        return cp

    for b in range(4):
        send1[0, b] = chip_sum(0, b).astype(bf)
    relay = [
        push(send1.at[0, pl.ds(0, 2)], rl_lo, s1.at[0], r1.at[0], dev(1, 0)),
        push(send1.at[0, pl.ds(2, 2)], rl_hi, s1.at[1], r1.at[1], dev(-1, 0)),
    ]
    for b in (2, 3):
        send1[1, b] = chip_sum(1, b).astype(bf)
    right = [push(send1.at[1, pl.ds(2, 2)], from_l.at[pl.ds(2, 2)], s1.at[2], r1.at[2], dev(1, 0))]
    for b in (0, 1):
        send1[2, b] = chip_sum(2, b).astype(bf)
    left = [push(send1.at[2, pl.ds(0, 2)], from_r.at[pl.ds(0, 2)], s1.at[3], r1.at[3], dev(-1, 0))]
    relay[0].wait_recv()
    for b in (0, 1):
        send1[1, b] = (chip_sum(1, b) + rl_lo[b].astype(f32)).astype(bf)
    right.append(push(send1.at[1, pl.ds(0, 2)], from_l.at[pl.ds(0, 2)], s1.at[4], r1.at[4], dev(1, 0)))
    relay[1].wait_recv()
    for b in (2, 3):
        send1[2, b] = (chip_sum(2, b) + rl_hi[b - 2].astype(f32)).astype(bf)
    left.append(push(send1.at[2, pl.ds(2, 2)], from_r.at[pl.ds(2, 2)], s1.at[5], r1.at[5], dev(-1, 0)))
    for b in range(4):
        mid[b] = chip_sum(3, b)
    for cp in right + left:
        cp.wait_recv()
    stage2 = []
    for j, d in enumerate((2, 1, -1)):
        b = wrap(b0 + d)
        send2[j] = (mid[b] + from_l[b].astype(f32) + from_r[b].astype(f32)).astype(bf)
        stage2.append(push(send2.at[j], recv2.at[j], s2.at[j], r2.at[j], dev(0, d)))
    tot = mid[b0] + from_l[b0].astype(f32) + from_r[b0].astype(f32)
    for cp in stage2:
        cp.wait_recv()
    tot = tot + recv2[0].astype(f32) + recv2[1].astype(f32) + recv2[2].astype(f32)
    fin[...] = tot.astype(bf)
    last = push(fin.at[pl.ds(pl.multiple_of((1 - c) * 256, 256), 256)], kvo.at[c], s3, r3, partner)
    keep = pltpu.make_async_copy(fin.at[pl.ds(pl.multiple_of(c * 256, 256), 256)], kvo.at[c], lsem.at[16])
    keep.start()

    for cp in relay + right + left + stage2 + exch:
        cp.wait_send()
    last.wait_send()
    pltpu.make_async_copy(fin.at[pl.ds(0, 256)], kvo.at[1 - c], r3).wait()
    keep.wait()
    pltpu.make_async_copy(dqo, dqo, dqrecv).wait()
    for mine, rem in moves:

        @pl.when(jnp.logical_not(mine))
        def _():
            rem.wait_send()


def reduce(dq, dkv):
    bf, f32 = jnp.bfloat16, jnp.float32
    dma = pltpu.SemaphoreType.DMA
    vm = pltpu.VMEM
    return pl.pallas_call(
        reduce_kernel,
        out_shape=(
            jax.ShapeDtypeStruct((20, 2, 64, 128), bf),
            jax.ShapeDtypeStruct((2, 256, 128), bf),
        ),
        in_specs=[ANY] * 2,
        out_specs=(ANY,) * 2,
        scratch_shapes=[
            vm((4, 4, 512, 128), bf), vm((4, 4, 512, 128), bf), vm((3, 4, 512, 128), bf), vm((4, 512, 128), f32),
            vm((2, 512, 128), bf), vm((2, 512, 128), bf), vm((4, 512, 128), bf), vm((4, 512, 128), bf),
            vm((3, 512, 128), bf), vm((3, 512, 128), bf), vm((512, 128), bf),
            dma((20,)), dma, dma((16,)), dma((16,)), dma((6,)), dma((6,)), dma((3,)), dma((3,)), dma, dma, dma((17,)),
        ],
        compiler_params=pltpu.CompilerParams(collective_id=1, has_side_effects=True),
        name="reduce_grads",
    )(dq, dkv)


def per_device(queries, grad_out, keys, values, doc_start):
    qh = jnp.transpose(queries, (2, 0, 1, 3))
    gh = jnp.transpose(grad_out, (2, 0, 1, 3))
    qbuf, gbuf, kfull, vfull = gather(qh, gh, keys.reshape(256, 128), values.reshape(256, 128))
    dq, dkv = attn(
        doc_start,
        qbuf.reshape(ROUNDS, 256, 128),
        gbuf.reshape(ROUNDS, 256, 128),
        kfull.reshape(8192, 128),
        vfull.reshape(8192, 128),
    )
    dqo, kvo = reduce(dq.reshape(ROUNDS, 2, 128, 128), dkv.reshape(2, 4, 4, 512, 128))
    query_grads = jnp.transpose(dqo, (1, 2, 0, 3))
    return query_grads, kvo[0].reshape(256, 1, 128), kvo[1].reshape(256, 1, 128)


def solution(mesh):
    in_specs = (
        P(None, ("seq", "head"), None, None),
        P(None, ("seq", "head"), None, None),
        P("seq", "head", None),
        P("seq", "head", None),
        P(),
    )
    out_specs = (
        P(None, ("seq", "head"), None, None),
        P("seq", "head", None),
        P("seq", "head", None),
    )
    return jax.shard_map(per_device, mesh=mesh, in_specs=in_specs, out_specs=out_specs, check_vma=False)
```

time: 603 us -> 141 us (0.23)
  waiting for transfers between devices: 471 us -> 0 us
  Pallas kernels: 0 us -> 131 us
  matrix products: 32.5 us -> 0 us
  other arithmetic: 20.2 us -> 0 us
  loops' own time: 19.6 us -> 0 us
  blocking collectives: 14.3 us -> 0 us
  between operations: 13.9 us -> 0.65 us
  local copies, waits for them, and re-layouts: 16 us -> 5.98 us
  starting transfers between devices: 9.71 us -> 0 us
    reduce_scatter x2 -> x0, waiting for transfers between devices: 391 us -> none  [the longest x1 307 us: layer_pass(): lax.psum_scatter(value_buffer, 'seq', scatter_dimension=0, tiled=True)]
    pallas_call x0 -> x3, Pallas kernels: none -> 131 us  [the longest x1 56.2 us: gather(): pl.pallas_call(gather_kernel, out_shape=(jax.ShapeDtypeStruct((ROUNDS, 2,...]
    all_gather x2 -> x0, waiting for transfers between devices: 63.4 us -> none  [the longest x1 45.1 us: layer_pass(): lax.all_gather(values, 'seq', axis=0, tiled=True)]
    dot_general x14 -> x0, matrix products: 32.5 us -> none  [the longest x4 7.4 us: masked_scores(): jnp.einsum('lrkgd,nkd->lkgrn', query_rows, key_block, preferred_element_t...]
    another operation x36 -> x0, loops' own time: 19.6 us -> none  [the longest x4 18.5 us: over_blocks(): return lax.fori_loop(0, key_count // block_rows, one_block, carried)]
    all_to_all x2 -> x0, waiting for transfers between devices: 15.4 us -> none  [the longest x1 8.04 us: per_device(): lax.all_to_all(queries, 'head', split_axis=2, concat_axis=1, tiled=True)]
    all_to_all x1 -> x0, blocking collectives: 14.3 us -> none  [per_device(): lax.all_to_all(query_final, 'head', split_axis=1, concat_axis=2, tiled=True)]
    add x12 -> x0, other arithmetic: 11.7 us -> none  [the longest x2 11.7 us: per_device(): key_total, value_total = (key_total + key_own, value_total + value_own)]
  transfers between devices with their start and end apart: 6 -> 0, of which waited for: 6 -> 0; matrix products, arithmetic and copies ran while one was open for 3% -> 0% of each run, Pallas kernels for 0% -> 0%
where the time goes in v1:
time: 141 us; the launch traced here: 138 us
  Pallas kernels  131 us (93%)
  local copies, waits for them, and re-layouts  5.98 us (4%)
    pallas_call x1, Pallas kernels, gather(): pl.pallas_call(gather_kernel, out_shape=(jax.ShapeDtypeStruct((ROUNDS, 2,...  56.2 us
    pallas_call x1, Pallas kernels, attn(): pl.pallas_call(attn_kernel, out_shape=(jax.ShapeDtypeStruct((ROUNDS, 256,...  43.6 us
    pallas_call x1, Pallas kernels, reduce(): pl.pallas_call(reduce_kernel, out_shape=(jax.ShapeDtypeStruct((20, 2, 64,...  31.6 us

profile of v1, /device:TPU:1, one launch (start us, length us, event | category | flops | bytes accessed | tf_op | source)
XLA Modules:
  0.0 138.1 jit_solution(9007782119221146442)
XLA Ops:
  0.6 2.5 %copy_bitcast_fusion = (bf16[20,2,64,128]{3,2,1,0:T(8,128)(2,1)}, bf16[20,2,64,128]{3,2,1,0:T(8,128)(2,1)}) fusion(bf16[2,64,20,128]{3,1,2,0:T(8,128)(2,1)} %param.6, bf16[2,64,20,128]{3,1,2,0:T(8,128)(2,1)} %param.5), kind=kLoop, calls=%fused_computation | loop fusion | bytes 2621440 | tf_op jit(solution)/shard_map/transpose | solution.py:473
  3.1 56.2 %gather_units.1 = (bf16[10,2,128,128]{3,2,1,0:T(8,128)(2,1)}, bf16[10,2,128,128]{3,2,1,0:T(8,128)(2,1)}, bf16[32,256,128]{2,1,0:T(8,128)(2,1)}, bf16[32,256,128]{2,1,0:T(8,128)(2,1)}) custom-call(bf16[20,2,64,128]{3,2,1,0:T(8,128)(2,1)} %get-tuple-element.25.qh, bf16[20,2,64,128]{3,2,1,0:T(8,128)(2,1)} %get-tuple-element.24.gh, bf16[256,128]{1,0:T(8,128)(2,1)} %bitcast.26, ...), custom_call_target="tpu_custom_call" | custom-call | tf_op jit(solution)/shard_map/gather_units/pallas_call | solution.py:203
  59.3 43.6 %attn_grads.1 = (bf16[10,256,128]{2,1,0:T(8,128)(2,1)}, bf16[2,8192,128]{2,1,0:T(8,128)(2,1)}) custom-call(s32[8192]{0:T(1024)} %doc_s.1, s32[64,128]{1,0:T(8,128)} %bitcast.25, bf16[10,256,128]{2,1,0:T(8,128)(2,1)} %bitcast.23, bf16[10,256,128]{2,1,0:T(8,128)(2,1)} %bitcast.24, bf16[8192,128]{1,0:T(8,128)(2,1)} %bitcast.19, bf16[8192,128]{1,0:T(8,128)(2,1)} %bitcast.20), custom_call_target="tpu_custom_call" | custom-call | tf_op jit(solution)/shard_map/attn_grads/pallas_call | solution.py:289
  102.9 31.6 %reduce_grads.1 = (bf16[20,2,64,128]{3,2,1,0:T(8,128)(2,1)}, bf16[2,256,128]{2,1,0:T(8,128)(2,1)}) custom-call(bf16[10,2,128,128]{3,2,1,0:T(8,128)(2,1)} %bitcast.21, bf16[2,4,4,512,128]{4,3,2,1,0:T(8,128)(2,1)} %bitcast.18), custom_call_target="tpu_custom_call" | custom-call | tf_op jit(solution)/shard_map/reduce_grads/pallas_call | solution.py:452
  134.5 2.0 %copy.10 = bf16[2,64,20,128]{3,1,2,0:T(8,128)(2,1)} copy(bf16[2,64,20,128]{3,1,0,2:T(8,128)(2,1)} %bitcast.22) | data formatting | bytes 1310720
  136.5 1.5 %slice_bitcast_fusion = (bf16[256,1,128]{2,0,1:T(8,128)(2,1)}, bf16[256,1,128]{2,0,1:T(8,128)(2,1)}) fusion(bf16[2,256,128]{2,1,0:T(8,128)(2,1)} %get-tuple-element.18), kind=kLoop, calls=%fused_computation.2 | loop fusion | bytes 262144 | tf_op jit(solution)/shard_map/reshape;squeeze | solution.py:484

commit v2 on v1

--- a/solution.py
+++ b/solution.py
@@ -11,6 +11,8 @@
 NEG = -1e30
 ROUNDS = 10
 BK = 1024
+CH = 256
+FIRST, PACE = 2, 2
 MESH = pl.DeviceIdType.MESH
 NT = (((1,), (1,)), ((), ()))
 TN = (((0,), (0,)), ((), ()))
@@ -38,11 +40,13 @@
 def unit_dest(n):
     r = n // 32
     p = lax.rem(n, 32)
-    return r, jnp.where(lax.rem(r, 2) == 0, p, 31 - p)
+    p = jnp.where(lax.rem(r, 2) == 0, p, 31 - p)
+    return r, seq_of(lax.rem(p, 4), lax.rem(p // 4, 4), p // 16)
 
 
 def unit_at(r, s):
-    return 32 * r + jnp.where(lax.rem(r, 2) == 0, s, 31 - s)
+    p = s // 8 + 4 * lax.rem(s // 2, 4) + 16 * lax.rem(s, 2)
+    return 32 * r + jnp.where(lax.rem(r, 2) == 0, p, 31 - p)
 
 
 def at_dev(s, z):
@@ -161,7 +165,9 @@
     vstep(0, 0)
 
     moves = []
-    for i, (h, g, r, ds) in enumerate(dests):
+
+    def unit_move(i):
+        h, g, r, ds = dests[i]
         mine = jnp.logical_and(ds == s, g == z)
         for srcs, buf, snd, rcv in ((qh, qbuf, qsend, qrecv), (gh, gbuf, gsend, grecv)):
             src = srcs.at[g * 5 + h]
@@ -180,7 +186,11 @@
 
             moves.append((mine, rem))
 
-    for da, db in order[1:]:
+    nxt = 0
+    for j, (da, db) in enumerate(order[1:]):
+        while nxt < min(20, FIRST + j * PACE):
+            unit_move(nxt)
+            nxt += 1
         kstep(da, db)
         vstep(da, db)
     kfin()
@@ -208,7 +218,7 @@
             jax.ShapeDtypeStruct((32, 256, 128), bf),
             jax.ShapeDtypeStruct((32, 256, 128), bf),
         ),
-        in_specs=[ANY] * 4,
+        in_specs=[ANY, ANY, VM, VM],
         out_specs=(ANY,) * 4,
         scratch_shapes=[dma((20,)), dma((20,)), dma, dma, dma((40,)), dma((40,)), dma((32,)), dma((32,)), dma((32,)), dma((32,)), dma((2,))],
         compiler_params=pltpu.CompilerParams(collective_id=0, has_side_effects=True),
@@ -217,72 +227,112 @@
 
 
 def attn_kernel(doc_s, doc_v, q_ref, g_ref, k_ref, v_ref, dq_ref, dkv_ref, s_scr, p_scr, dk_acc, dv_acc):
+    f32, bf = jnp.float32, jnp.bfloat16
     scale = 1.0 / math.sqrt(128)
     c = scale * math.log2(math.e)
     sidx = lax.axis_index("seq")
-    dk_acc[...] = jnp.zeros_like(dk_acc)
-    dv_acc[...] = jnp.zeros_like(dv_acc)
+
+    def zero(i, _):
+        rows = pl.ds(pl.multiple_of(i * 256, 256), 256)
+        dk_acc[rows, :] = jnp.zeros((256, 128), f32)
+        dv_acc[rows, :] = jnp.zeros((256, 128), f32)
+        return 0
+
+    lax.fori_loop(0, 32, zero, 0)
+
+    def split(x):
+        return x.reshape(CH // 8, 8, 256)
 
     def tile(r, _):
-        first = (unit_at(r, sidx) // 5) * 128
+        b = unit_at(r, sidx) // 5
+        first = b * 128
         last = first + 127
-        start_min = doc_s[first]
         start_max = doc_s[last]
-        lo = start_min // BK
+        lo = doc_s[first] // BK
         hi = last // BK + 1
-        fhi = jnp.minimum((first + 1) // BK, hi)
-        flo = jnp.minimum(jnp.maximum(lo, (start_max + BK - 1) // BK), hi)
-        fhi = jnp.maximum(fhi, flo)
-        srow = doc_v[pl.ds(unit_at(r, sidx) // 5, 1), :]
+        flo = jnp.clip((start_max + BK - 1) // BK, lo + 1, hi)
+        fhi = jnp.clip((first + 1) // BK, flo, hi)
+        srow = doc_v[pl.ds(b, 1), :]
         prow = first + lax.broadcasted_iota(jnp.int32, (1, 128), 1)
         srow = jnp.concatenate([srow, srow], axis=1)
         prow = jnp.concatenate([prow, prow], axis=1)
         q = q_ref[r]
         g = g_ref[r]
 
-        def stats(masked, kb, carry):
-            m, l, w = carry
+        def produce(masked, o, j, mx):
+            start = pl.multiple_of(o + j * CH, CH)
+            rows = pl.ds(start, CH)
+            s = lax.dot_general(k_ref[rows, :], q, NT, preferred_element_type=f32)
+            dp = lax.dot_general(v_ref[rows, :], g, NT, preferred_element_type=f32)
+            if masked:
+                kp = start + lax.broadcasted_iota(jnp.int32, (CH, 256), 0)
+                s = jnp.where((kp >= srow) & (kp <= prow), s, NEG)
+            s_scr[rows, :] = s
+            p_scr[rows, :] = dp
+            return jnp.maximum(mx, jnp.max(split(s), axis=0))
+
+        def consume(o, j, mn, l, w):
+            rows = pl.ds(pl.multiple_of(o + j * CH, CH), CH)
+            e = jnp.exp2((split(s_scr[rows, :]) - mn) * c)
+            return l + jnp.sum(e, axis=0), w + jnp.sum(e * split(p_scr[rows, :]), axis=0)
+
+        neg = jnp.full((8, 256), NEG, f32)
+        zeros = jnp.zeros((8, 256), f32)
+        mx = neg
+        for j in range(BK // CH):
+            mx = produce(True, lo * BK, j, mx)
+
+        def body(masked, kb, carry):
+            m, l, w, mx = carry
+            a = jnp.exp2((m - mx) * c)
+            l, w = l * a, w * a
+            nx = mx
             o = pl.multiple_of(kb * BK, BK)
-            s = lax.dot_general(k_ref[pl.ds(o, BK), :], q, NT, preferred_element_type=jnp.float32)
-            dp = lax.dot_general(v_ref[pl.ds(o, BK), :], g, NT, preferred_element_type=jnp.float32)
-            if masked:
-                kp = o + lax.broadcasted_iota(jnp.int32, (BK, 256), 0)
-                s = jnp.where((kp >= srow) & (kp <= prow), s, NEG)
-            s_scr[pl.ds(o, BK), :] = s
-            p_scr[pl.ds(o, BK), :] = dp
-            mn = jnp.maximum(m, jnp.max(s, axis=0, keepdims=True))
-            a = jnp.exp2((m - mn) * c)
-            e = jnp.exp2((s - mn) * c)
-            l = l * a + jnp.sum(e, axis=0, keepdims=True)
-            w = w * a + jnp.sum(e * dp, axis=0, keepdims=True)
-            return mn, l, w
-
-        zero = jnp.zeros((1, 256), jnp.float32)
-        carry = (zero + NEG, zero, zero)
-        carry = lax.fori_loop(lo, flo, functools.partial(stats, True), carry)
-        carry = lax.fori_loop(flo, fhi, functools.partial(stats, False), carry)
-        m, l, w = lax.fori_loop(fhi, hi, functools.partial(stats, True), carry)
-        shift = m * c + jnp.log2(l)
-        delta = w / l
+            for j in range(BK // CH):
+                l, w = consume(o - BK, j, mx, l, w)
+                nx = produce(masked, o, j, nx)
+            return mx, l, w, nx
+
+        carry = (neg, zeros, zeros, mx)
+        carry = lax.fori_loop(lo + 1, flo, functools.partial(body, True), carry)
+        carry = lax.fori_loop(flo, fhi, functools.partial(body, False), carry)
+        m, l, w, mx = lax.fori_loop(fhi, hi, functools.partial(body, True), carry)
+        a = jnp.exp2((m - mx) * c)
+        l, w = l * a, w * a
+        for j in range(BK // CH):
+            l, w = consume((hi - 1) * BK, j, mx, l, w)
+        top = jnp.max(mx, axis=0, keepdims=True)
+        a = jnp.exp2((mx - top) * c)
+        l = jnp.sum(l * a, axis=0, keepdims=True)
+        w = jnp.sum(w * a, axis=0, keepdims=True)
+        shift = jnp.broadcast_to(top * c + jnp.log2(l), (8, 256))
+        delta = jnp.broadcast_to(w / l, (8, 256))
 
         def grads(kb, acc):
-            o = pl.multiple_of(kb * BK, BK)
-            rows = pl.ds(o, BK)
-            p = jnp.exp2(s_scr[rows, :] * c - shift)
-            ds = p * (p_scr[rows, :] - delta)
-            p16 = p.astype(jnp.bfloat16)
-            d16 = ds.astype(jnp.bfloat16)
-            dv_acc[rows, :] += jnp.dot(p16, g, preferred_element_type=jnp.float32)
-            dk_acc[rows, :] += jnp.dot(d16, q, preferred_element_type=jnp.float32)
-            return acc + lax.dot_general(d16, k_ref[rows, :], TN, preferred_element_type=jnp.float32)
-
-        acc = lax.fori_loop(lo, hi, grads, jnp.zeros((256, 128), jnp.float32))
-        dq_ref[r] = (acc * scale).astype(jnp.bfloat16)
+            for j in range(BK // CH):
+                rows = pl.ds(pl.multiple_of(kb * BK + j * CH, CH), CH)
+                p = jnp.exp2(split(s_scr[rows, :]) * c - shift)
+                ds = p * (split(p_scr[rows, :]) - delta)
+                p16 = p.reshape(CH, 256).astype(bf)
+                d16 = ds.reshape(CH, 256).astype(bf)
+                dv_acc[rows, :] += jnp.dot(p16, g, preferred_element_type=f32)
+                dk_acc[rows, :] += jnp.dot(d16, q, preferred_element_type=f32)
+                acc = acc + lax.dot_general(d16, k_ref[rows, :], TN, preferred_element_type=f32)
+            return acc
+
+        acc = lax.fori_loop(lo, hi, grads, jnp.zeros((256, 128), f32))
+        dq_ref[r] = (acc * scale).astype(bf)
         return 0
 
     lax.fori_loop(0, ROUNDS, tile, 0)
-    dkv_ref[0] = (dk_acc[...] * scale).astype(jnp.bfloat16)
-    dkv_ref[1] = dv_acc[...].astype(jnp.bfloat16)
+
+    def put(i, _):
+        rows = pl.ds(pl.multiple_of(i * 256, 256), 256)
+        dkv_ref[0, rows, :] = (dk_acc[rows, :] * scale).astype(bf)
+        dkv_ref[1, rows, :] = dv_acc[rows, :].astype(bf)
+        return 0
+
+    lax.fori_loop(0, 32, put, 0)
 
 
 def attn(doc, q, g, k, v):

time: 141 us -> 127 us (0.901); the launches traced: 138 us -> 126 us
  Pallas kernels: 131 us -> 120 us
    pallas_call x1, Pallas kernels: 56.2 us -> 46.6 us  [gather(): pl.pallas_call(gather_kernel, out_shape=(jax.ShapeDtypeStruct((ROUNDS, 2,...]
    pallas_call x1, Pallas kernels: 43.6 us -> 37.4 us  [attn(): pl.pallas_call(attn_kernel, out_shape=(jax.ShapeDtypeStruct((ROUNDS, 256,...]
    pallas_call x1, Pallas kernels: 31.6 us -> 35.6 us  [reduce(): pl.pallas_call(reduce_kernel, out_shape=(jax.ShapeDtypeStruct((20, 2, 64,...]
where the time goes in v2:
time: 127 us; the launch traced here: 126 us
  Pallas kernels  120 us (94%)
  local copies, waits for them, and re-layouts  5.98 us (5%)
    pallas_call x1, Pallas kernels, gather(): pl.pallas_call(gather_kernel, out_shape=(jax.ShapeDtypeStruct((ROUNDS, 2,...  46.6 us
    pallas_call x1, Pallas kernels, attn(): pl.pallas_call(attn_kernel, out_shape=(jax.ShapeDtypeStruct((ROUNDS, 256,...  37.4 us
    pallas_call x1, Pallas kernels, reduce(): pl.pallas_call(reduce_kernel, out_shape=(jax.ShapeDtypeStruct((20, 2, 64,...  35.6 us

profile of v2, /device:TPU:1, one launch (start us, length us, event | category | flops | bytes accessed | tf_op | source)
XLA Modules:
  0.0 126.2 jit_solution(4354846021604107705)
XLA Ops:
  0.6 2.5 %copy_bitcast_fusion = (bf16[20,2,64,128]{3,2,1,0:T(8,128)(2,1)}, bf16[20,2,64,128]{3,2,1,0:T(8,128)(2,1)}) fusion(bf16[2,64,20,128]{3,1,2,0:T(8,128)(2,1)} %param.6, bf16[2,64,20,128]{3,1,2,0:T(8,128)(2,1)} %param.5), kind=kLoop, calls=%fused_computation | loop fusion | bytes 2621440 | tf_op jit(solution)/shard_map/transpose | solution.py:523
  3.1 46.6 %gather_units.1 = (bf16[10,2,128,128]{3,2,1,0:T(8,128)(2,1)}, bf16[10,2,128,128]{3,2,1,0:T(8,128)(2,1)}, bf16[32,256,128]{2,1,0:T(8,128)(2,1)}, bf16[32,256,128]{2,1,0:T(8,128)(2,1)}) custom-call(bf16[20,2,64,128]{3,2,1,0:T(8,128)(2,1)} %get-tuple-element.25.qh, bf16[20,2,64,128]{3,2,1,0:T(8,128)(2,1)} %get-tuple-element.24.gh, bf16[256,128]{1,0:T(8,128)(2,1)} %bitcast.26, ...), custom_call_target="tpu_custom_call" | custom-call | tf_op jit(solution)/shard_map/gather_units/pallas_call | solution.py:213
  49.7 37.4 %attn_grads.1 = (bf16[10,256,128]{2,1,0:T(8,128)(2,1)}, bf16[2,8192,128]{2,1,0:T(8,128)(2,1)}) custom-call(s32[8192]{0:T(1024)} %doc_s.1, s32[64,128]{1,0:T(8,128)} %bitcast.25, bf16[10,256,128]{2,1,0:T(8,128)(2,1)} %bitcast.23, bf16[10,256,128]{2,1,0:T(8,128)(2,1)} %bitcast.24, bf16[8192,128]{1,0:T(8,128)(2,1)} %bitcast.19, bf16[8192,128]{1,0:T(8,128)(2,1)} %bitcast.20), custom_call_target="tpu_custom_call" | custom-call | tf_op jit(solution)/shard_map/attn_grads/pallas_call | solution.py:339
  87.1 35.6 %reduce_grads.1 = (bf16[20,2,64,128]{3,2,1,0:T(8,128)(2,1)}, bf16[2,256,128]{2,1,0:T(8,128)(2,1)}) custom-call(bf16[10,2,128,128]{3,2,1,0:T(8,128)(2,1)} %bitcast.21, bf16[2,4,4,512,128]{4,3,2,1,0:T(8,128)(2,1)} %bitcast.18), custom_call_target="tpu_custom_call" | custom-call | tf_op jit(solution)/shard_map/reduce_grads/pallas_call | solution.py:502
  122.7 2.0 %copy.10 = bf16[2,64,20,128]{3,1,2,0:T(8,128)(2,1)} copy(bf16[2,64,20,128]{3,1,0,2:T(8,128)(2,1)} %bitcast.22) | data formatting | bytes 1310720
  124.7 1.5 %slice_bitcast_fusion = (bf16[256,1,128]{2,0,1:T(8,128)(2,1)}, bf16[256,1,128]{2,0,1:T(8,128)(2,1)}) fusion(bf16[2,256,128]{2,1,0:T(8,128)(2,1)} %get-tuple-element.18), kind=kLoop, calls=%fused_computation.2 | loop fusion | bytes 262144 | tf_op jit(solution)/shard_map/reshape;squeeze | solution.py:534

commit v3 on v2

--- a/solution.py
+++ b/solution.py
@@ -11,7 +11,7 @@
 NEG = -1e30
 ROUNDS = 10
 BK = 1024
-CH = 256
+SB, CH, GC = 256, 64, 128
 FIRST, PACE = 2, 2
 MESH = pl.DeviceIdType.MESH
 NT = (((1,), (1,)), ((), ()))
@@ -226,11 +226,14 @@
     )(qh, gh, k, v)
 
 
-def attn_kernel(doc_s, doc_v, q_ref, g_ref, k_ref, v_ref, dq_ref, dkv_ref, s_scr, p_scr, dk_acc, dv_acc):
+def attn_kernel(doc_s, doc_v, q_ref, g_ref, k_ref, v_ref, dq_ref, dkv_ref, s0, p0, s1, p1, dk_acc, dv_acc):
     f32, bf = jnp.float32, jnp.bfloat16
     scale = 1.0 / math.sqrt(128)
     c = scale * math.log2(math.e)
     sidx = lax.axis_index("seq")
+    scratch = ((s0, p0), (s1, p1))
+    neg = jnp.full((8, 256), NEG, f32)
+    zeros = jnp.zeros((8, 256), f32)
 
     def zero(i, _):
         rows = pl.ds(pl.multiple_of(i * 256, 256), 256)
@@ -241,90 +244,120 @@
     lax.fori_loop(0, 32, zero, 0)
 
     def split(x):
-        return x.reshape(CH // 8, 8, 256)
-
-    def tile(r, _):
+        return x.reshape(x.shape[0] // 8, 8, 256)
+
+    def info(r):
         b = unit_at(r, sidx) // 5
         first = b * 128
-        last = first + 127
-        start_max = doc_s[last]
-        lo = doc_s[first] // BK
-        hi = last // BK + 1
-        flo = jnp.clip((start_max + BK - 1) // BK, lo + 1, hi)
-        fhi = jnp.clip((first + 1) // BK, flo, hi)
+        start_max = doc_s[first + 127]
+        lo = (doc_s[first] // 128) * 128
+        hi = first + 128
+        count = (hi - lo + BK - 1) // BK
+        base = jnp.maximum(hi - count * BK, 0)
+        flo = jnp.clip((start_max - base + BK - 1) // BK, 0, count)
+        fhi = jnp.clip((first + 1 - base) // BK, flo, count)
+        return b, first, count, base, flo, fhi
+
+    def spans(b, first):
         srow = doc_v[pl.ds(b, 1), :]
         prow = first + lax.broadcasted_iota(jnp.int32, (1, 128), 1)
-        srow = jnp.concatenate([srow, srow], axis=1)
-        prow = jnp.concatenate([prow, prow], axis=1)
-        q = q_ref[r]
-        g = g_ref[r]
-
-        def produce(masked, o, j, mx):
-            start = pl.multiple_of(o + j * CH, CH)
-            rows = pl.ds(start, CH)
-            s = lax.dot_general(k_ref[rows, :], q, NT, preferred_element_type=f32)
-            dp = lax.dot_general(v_ref[rows, :], g, NT, preferred_element_type=f32)
-            if masked:
-                kp = start + lax.broadcasted_iota(jnp.int32, (CH, 256), 0)
-                s = jnp.where((kp >= srow) & (kp <= prow), s, NEG)
-            s_scr[rows, :] = s
-            p_scr[rows, :] = dp
-            return jnp.maximum(mx, jnp.max(split(s), axis=0))
-
-        def consume(o, j, mn, l, w):
-            rows = pl.ds(pl.multiple_of(o + j * CH, CH), CH)
-            e = jnp.exp2((split(s_scr[rows, :]) - mn) * c)
-            return l + jnp.sum(e, axis=0), w + jnp.sum(e * split(p_scr[rows, :]), axis=0)
-
-        neg = jnp.full((8, 256), NEG, f32)
-        zeros = jnp.zeros((8, 256), f32)
-        mx = neg
-        for j in range(BK // CH):
-            mx = produce(True, lo * BK, j, mx)
-
-        def body(masked, kb, carry):
-            m, l, w, mx = carry
-            a = jnp.exp2((m - mx) * c)
-            l, w = l * a, w * a
-            nx = mx
-            o = pl.multiple_of(kb * BK, BK)
-            for j in range(BK // CH):
-                l, w = consume(o - BK, j, mx, l, w)
-                nx = produce(masked, o, j, nx)
-            return mx, l, w, nx
-
-        carry = (neg, zeros, zeros, mx)
-        carry = lax.fori_loop(lo + 1, flo, functools.partial(body, True), carry)
-        carry = lax.fori_loop(flo, fhi, functools.partial(body, False), carry)
-        m, l, w, mx = lax.fori_loop(fhi, hi, functools.partial(body, True), carry)
-        a = jnp.exp2((m - mx) * c)
-        l, w = l * a, w * a
-        for j in range(BK // CH):
-            l, w = consume((hi - 1) * BK, j, mx, l, w)
-        top = jnp.max(mx, axis=0, keepdims=True)
-        a = jnp.exp2((mx - top) * c)
+        return jnp.concatenate([srow, srow], axis=1), jnp.concatenate([prow, prow], axis=1)
+
+    def stats(r, par, base, span, masked, t, carry):
+        m, l, w = carry
+        s_scr, p_scr = scratch[par]
+        o = base + t * BK
+        for h in range(BK // SB):
+            rows = pl.ds(pl.multiple_of(o + h * SB, 128), SB)
+            s = lax.dot_general(k_ref[rows, :], q_ref[r], NT, preferred_element_type=f32)
+            dp = lax.dot_general(v_ref[rows, :], g_ref[r], NT, preferred_element_type=f32)
+            for j in range(SB // CH):
+                part = slice(j * CH, (j + 1) * CH)
+                start = pl.multiple_of(o + h * SB + j * CH, CH)
+                sj, dj = s[part], dp[part]
+                if masked:
+                    kp = start + lax.broadcasted_iota(jnp.int32, (CH, 256), 0)
+                    sj = jnp.where((kp >= span[0]) & (kp <= span[1]), sj, NEG)
+                s_scr[pl.ds(start, CH), :] = sj
+                p_scr[pl.ds(start, CH), :] = dj
+                sj, dj = split(sj), split(dj)
+                top = jnp.maximum(m, jnp.max(sj, axis=0))
+                a = jnp.exp2((m - top) * c)
+                e = jnp.exp2((sj - top) * c)
+                l = l * a + jnp.sum(e, axis=0)
+                w = w * a + jnp.sum(e * dj, axis=0)
+                m = top
+                yield m, l, w
+
+    def finish(carry):
+        m, l, w = carry
+        top = jnp.max(m, axis=0, keepdims=True)
+        a = jnp.exp2((m - top) * c)
         l = jnp.sum(l * a, axis=0, keepdims=True)
         w = jnp.sum(w * a, axis=0, keepdims=True)
-        shift = jnp.broadcast_to(top * c + jnp.log2(l), (8, 256))
-        delta = jnp.broadcast_to(w / l, (8, 256))
-
-        def grads(kb, acc):
-            for j in range(BK // CH):
-                rows = pl.ds(pl.multiple_of(kb * BK + j * CH, CH), CH)
-                p = jnp.exp2(split(s_scr[rows, :]) * c - shift)
-                ds = p * (split(p_scr[rows, :]) - delta)
-                p16 = p.reshape(CH, 256).astype(bf)
-                d16 = ds.reshape(CH, 256).astype(bf)
-                dv_acc[rows, :] += jnp.dot(p16, g, preferred_element_type=f32)
-                dk_acc[rows, :] += jnp.dot(d16, q, preferred_element_type=f32)
-                acc = acc + lax.dot_general(d16, k_ref[rows, :], TN, preferred_element_type=f32)
-            return acc
-
-        acc = lax.fori_loop(lo, hi, grads, jnp.zeros((256, 128), f32))
+        return jnp.broadcast_to(top * c + jnp.log2(l), (8, 256)), jnp.broadcast_to(w / l, (8, 256))
+
+    def grads(r, par, base, fin, t, acc):
+        s_scr, p_scr = scratch[par]
+        shift, delta = fin
+        for j in range(BK // GC):
+            rows = pl.ds(pl.multiple_of(base + t * BK + j * GC, 128), GC)
+            p = jnp.exp2(split(s_scr[rows, :]) * c - shift)
+            ds = p * (split(p_scr[rows, :]) - delta)
+            p16 = p.reshape(GC, 256).astype(bf)
+            d16 = ds.reshape(GC, 256).astype(bf)
+            dv_acc[rows, :] += jnp.dot(p16, g_ref[r], preferred_element_type=f32)
+            dk_acc[rows, :] += jnp.dot(d16, q_ref[r], preferred_element_type=f32)
+            acc = acc + lax.dot_general(d16, k_ref[rows, :], TN, preferred_element_type=f32)
+            yield acc
+
+    def last(steps):
+        for out in steps:
+            pass
+        return out
+
+    def stats_loop(r, par, inf, span, t0, carry):
+        def body(t, carry):
+            return lax.cond(
+                jnp.logical_and(t >= inf[4], t < inf[5]),
+                lambda cc: last(stats(r, par, inf[3], span, False, t, cc)),
+                lambda cc: last(stats(r, par, inf[3], span, True, t, cc)),
+                carry,
+            )
+
+        return lax.fori_loop(t0, inf[2], body, carry)
+
+    def step(r, par, fin):
+        inf = info(r)
+        nxt = jnp.minimum(r + 1, ROUNDS - 1)
+        ninf = info(nxt)
+        ninf = ninf[:2] + (jnp.where(r + 1 < ROUNDS, ninf[2], 0),) + ninf[3:]
+        span = spans(ninf[0], ninf[1])
+        both = jnp.minimum(inf[2], ninf[2])
+
+        def body(t, carry):
+            def run(masked):
+                def go(cc):
+                    acc, st = cc
+                    side = grads(r, par, inf[3], fin, t, acc)
+                    for i, st in enumerate(stats(nxt, 1 - par, ninf[3], span, masked, t, st)):
+                        if (i + 1) % (GC // CH) == 0:
+                            acc = next(side)
+                    return acc, st
+
+                return go
+
+            return lax.cond(jnp.logical_and(t >= ninf[4], t < ninf[5]), run(False), run(True), carry)
+
+        acc, st = lax.fori_loop(0, both, body, (jnp.zeros((256, 128), f32), (neg, zeros, zeros)))
+        acc = lax.fori_loop(both, inf[2], lambda t, a: last(grads(r, par, inf[3], fin, t, a)), acc)
+        st = stats_loop(nxt, 1 - par, ninf, span, both, st)
         dq_ref[r] = (acc * scale).astype(bf)
-        return 0
-
-    lax.fori_loop(0, ROUNDS, tile, 0)
+        return finish(st)
+
+    inf0 = info(0)
+    fin = finish(stats_loop(0, 0, inf0, spans(inf0[0], inf0[1]), 0, (neg, zeros, zeros)))
+    lax.fori_loop(0, ROUNDS // 2, lambda i, fin: step(2 * i + 1, 1, step(2 * i, 0, fin)), fin)
 
     def put(i, _):
         rows = pl.ds(pl.multiple_of(i * 256, 256), 256)
@@ -344,12 +377,7 @@
         ),
         in_specs=[pl.BlockSpec(memory_space=pltpu.SMEM), VM, VM, VM, VM, VM],
         out_specs=(VM, VM),
-        scratch_shapes=[
-            pltpu.VMEM((8192, 256), jnp.float32),
-            pltpu.VMEM((8192, 256), jnp.float32),
-            pltpu.VMEM((8192, 128), jnp.float32),
-            pltpu.VMEM((8192, 128), jnp.float32),
-        ],
+        scratch_shapes=[pltpu.VMEM((8192, 256), jnp.float32)] * 4 + [pltpu.VMEM((8192, 128), jnp.float32)] * 2,
         compiler_params=pltpu.CompilerParams(vmem_limit_bytes=62 << 20),
         name="attn_grads",
     )(doc, doc.reshape(64, 128), q, g, k, v)

time: 127 us -> 120 us (0.945)
  Pallas kernels: 120 us -> 112 us
    pallas_call x1, Pallas kernels: 37.4 us -> 30.1 us  [attn(): pl.pallas_call(attn_kernel, out_shape=(jax.ShapeDtypeStruct((ROUNDS, 256,...]
where the time goes in v3:
time: 120 us; the launch traced here: 118 us
  Pallas kernels  112 us (93%)
  local copies, waits for them, and re-layouts  5.98 us (5%)
    pallas_call x1, Pallas kernels, gather(): pl.pallas_call(gather_kernel, out_shape=(jax.ShapeDtypeStruct((ROUNDS, 2,...  46.6 us
    pallas_call x1, Pallas kernels, reduce(): pl.pallas_call(reduce_kernel, out_shape=(jax.ShapeDtypeStruct((20, 2, 64,...  34.8 us
    pallas_call x1, Pallas kernels, attn(): pl.pallas_call(attn_kernel, out_shape=(jax.ShapeDtypeStruct((ROUNDS, 256,...  30.1 us
    transpose x1, local copies, waits for them, and re-layouts, per_device(): gh = jnp.transpose(grad_out, (2, 0, 1, 3))  2.48 us

profile of v3, /device:TPU:1, one launch (start us, length us, event | category | flops | bytes accessed | tf_op | source)
XLA Modules:
  0.0 118.1 jit_solution(18353904933818021618)
XLA Ops:
  0.6 2.5 %copy_bitcast_fusion = (bf16[20,2,64,128]{3,2,1,0:T(8,128)(2,1)}, bf16[20,2,64,128]{3,2,1,0:T(8,128)(2,1)}) fusion(bf16[2,64,20,128]{3,1,2,0:T(8,128)(2,1)} %param.6, bf16[2,64,20,128]{3,1,2,0:T(8,128)(2,1)} %param.5), kind=kLoop, calls=%fused_computation | loop fusion | bytes 2621440 | tf_op jit(solution)/shard_map/transpose | solution.py:551
  3.1 46.6 %gather_units.1 = (bf16[10,2,128,128]{3,2,1,0:T(8,128)(2,1)}, bf16[10,2,128,128]{3,2,1,0:T(8,128)(2,1)}, bf16[32,256,128]{2,1,0:T(8,128)(2,1)}, bf16[32,256,128]{2,1,0:T(8,128)(2,1)}) custom-call(bf16[20,2,64,128]{3,2,1,0:T(8,128)(2,1)} %get-tuple-element.25.qh, bf16[20,2,64,128]{3,2,1,0:T(8,128)(2,1)} %get-tuple-element.24.gh, bf16[256,128]{1,0:T(8,128)(2,1)} %bitcast.26, ...), custom_call_target="tpu_custom_call" | custom-call | tf_op jit(solution)/shard_map/gather_units/pallas_call | solution.py:213
  49.7 30.1 %attn_grads.1 = (bf16[10,256,128]{2,1,0:T(8,128)(2,1)}, bf16[2,8192,128]{2,1,0:T(8,128)(2,1)}) custom-call(s32[8192]{0:T(1024)} %doc_s.1, s32[64,128]{1,0:T(8,128)} %bitcast.25, bf16[10,256,128]{2,1,0:T(8,128)(2,1)} %bitcast.23, bf16[10,256,128]{2,1,0:T(8,128)(2,1)} %bitcast.24, bf16[8192,128]{1,0:T(8,128)(2,1)} %bitcast.19, bf16[8192,128]{1,0:T(8,128)(2,1)} %bitcast.20), custom_call_target="tpu_custom_call" | custom-call | tf_op jit(solution)/shard_map/attn_grads/pallas_call | solution.py:372
  79.8 34.8 %reduce_grads.1 = (bf16[20,2,64,128]{3,2,1,0:T(8,128)(2,1)}, bf16[2,256,128]{2,1,0:T(8,128)(2,1)}) custom-call(bf16[10,2,128,128]{3,2,1,0:T(8,128)(2,1)} %bitcast.21, bf16[2,4,4,512,128]{4,3,2,1,0:T(8,128)(2,1)} %bitcast.18), custom_call_target="tpu_custom_call" | custom-call | tf_op jit(solution)/shard_map/reduce_grads/pallas_call | solution.py:530
  114.6 2.0 %copy.10 = bf16[2,64,20,128]{3,1,2,0:T(8,128)(2,1)} copy(bf16[2,64,20,128]{3,1,0,2:T(8,128)(2,1)} %bitcast.22) | data formatting | bytes 1310720
  116.6 1.5 %slice_bitcast_fusion = (bf16[256,1,128]{2,0,1:T(8,128)(2,1)}, bf16[256,1,128]{2,0,1:T(8,128)(2,1)}) fusion(bf16[2,256,128]{2,1,0:T(8,128)(2,1)} %get-tuple-element.18), kind=kLoop, calls=%fused_computation.2 | loop fusion | bytes 262144 | tf_op jit(solution)/shard_map/reshape;squeeze | solution.py:562

commit v4 on v3

--- a/solution.py
+++ b/solution.py
@@ -11,7 +11,7 @@
 NEG = -1e30
 ROUNDS = 10
 BK = 1024
-SB, CH, GC = 256, 64, 128
+SB, CH, GC = 128, 64, 128
 FIRST, PACE = 2, 2
 MESH = pl.DeviceIdType.MESH
 NT = (((1,), (1,)), ((), ()))
@@ -226,7 +226,7 @@
     )(qh, gh, k, v)
 
 
-def attn_kernel(doc_s, doc_v, q_ref, g_ref, k_ref, v_ref, dq_ref, dkv_ref, s0, p0, s1, p1, dk_acc, dv_acc):
+def attn_kernel(doc_s, doc_v, q_hbm, g_hbm, k_hbm, v_hbm, dq_hbm, dkv_hbm, s0, p0, s1, p1, dk_acc, dv_acc, q_ref, g_ref, k_ref, v_ref, dq_ref, dkv_ref, in_sem, out_sem):
     f32, bf = jnp.float32, jnp.bfloat16
     scale = 1.0 / math.sqrt(128)
     c = scale * math.log2(math.e)
@@ -234,6 +234,17 @@
     scratch = ((s0, p0), (s1, p1))
     neg = jnp.full((8, 256), NEG, f32)
     zeros = jnp.zeros((8, 256), f32)
+
+    first_rows, rest = pl.ds(0, BK), pl.ds(BK, 8192 - BK)
+    pairs = ((q_hbm, q_ref), (g_hbm, g_ref), (k_hbm, k_ref), (v_hbm, v_ref))
+    early = [(a.at[pl.ds(0, 1)], b.at[pl.ds(0, 1)]) for a, b in pairs[:2]]
+    early += [(a.at[first_rows], b.at[first_rows]) for a, b in pairs[2:]]
+    late = [(a.at[pl.ds(1, ROUNDS - 1)], b.at[pl.ds(1, ROUNDS - 1)]) for a, b in pairs[:2]]
+    late += [(a.at[rest], b.at[rest]) for a, b in pairs[2:]]
+    early = [pltpu.make_async_copy(a, b, in_sem.at[i]) for i, (a, b) in enumerate(early)]
+    late = [pltpu.make_async_copy(a, b, in_sem.at[4 + i]) for i, (a, b) in enumerate(late)]
+    for cp in early + late:
+        cp.start()
 
     def zero(i, _):
         rows = pl.ds(pl.multiple_of(i * 256, 256), 256)
@@ -355,17 +366,30 @@
         dq_ref[r] = (acc * scale).astype(bf)
         return finish(st)
 
+    for cp in early:
+        cp.wait()
     inf0 = info(0)
     fin = finish(stats_loop(0, 0, inf0, spans(inf0[0], inf0[1]), 0, (neg, zeros, zeros)))
+    for cp in late:
+        cp.wait()
     lax.fori_loop(0, ROUNDS // 2, lambda i, fin: step(2 * i + 1, 1, step(2 * i, 0, fin)), fin)
 
-    def put(i, _):
-        rows = pl.ds(pl.multiple_of(i * 256, 256), 256)
-        dkv_ref[0, rows, :] = (dk_acc[rows, :] * scale).astype(bf)
-        dkv_ref[1, rows, :] = dv_acc[rows, :].astype(bf)
-        return 0
-
-    lax.fori_loop(0, 32, put, 0)
+    out = [pltpu.make_async_copy(dq_ref, dq_hbm, out_sem.at[8])]
+    out[0].start()
+    for n in range(8):
+
+        def put(i, _):
+            rows = pl.ds(pl.multiple_of(n * 1024 + i * 256, 256), 256)
+            dkv_ref[0, rows, :] = (dk_acc[rows, :] * scale).astype(bf)
+            dkv_ref[1, rows, :] = dv_acc[rows, :].astype(bf)
+            return 0
+
+        lax.fori_loop(0, 4, put, 0)
+        rows = pl.ds(n * 1024, 1024)
+        out.append(pltpu.make_async_copy(dkv_ref.at[:, rows], dkv_hbm.at[:, rows], out_sem.at[n]))
+        out[-1].start()
+    for cp in out:
+        cp.wait()
 
 
 def attn(doc, q, g, k, v):
@@ -375,9 +399,14 @@
             jax.ShapeDtypeStruct((ROUNDS, 256, 128), jnp.bfloat16),
             jax.ShapeDtypeStruct((2, 8192, 128), jnp.bfloat16),
         ),
-        in_specs=[pl.BlockSpec(memory_space=pltpu.SMEM), VM, VM, VM, VM, VM],
-        out_specs=(VM, VM),
-        scratch_shapes=[pltpu.VMEM((8192, 256), jnp.float32)] * 4 + [pltpu.VMEM((8192, 128), jnp.float32)] * 2,
+        in_specs=[pl.BlockSpec(memory_space=pltpu.SMEM), VM, ANY, ANY, ANY, ANY],
+        out_specs=(ANY, ANY),
+        scratch_shapes=[pltpu.VMEM((8192, 256), jnp.float32)] * 4
+        + [pltpu.VMEM((8192, 128), jnp.float32)] * 2
+        + [pltpu.VMEM((ROUNDS, 256, 128), jnp.bfloat16)] * 2
+        + [pltpu.VMEM((8192, 128), jnp.bfloat16)] * 2
+        + [pltpu.VMEM((ROUNDS, 256, 128), jnp.bfloat16), pltpu.VMEM((2, 8192, 128), jnp.bfloat16)]
+        + [pltpu.SemaphoreType.DMA((8,)), pltpu.SemaphoreType.DMA((9,))],
         compiler_params=pltpu.CompilerParams(vmem_limit_bytes=62 << 20),
         name="attn_grads",
     )(doc, doc.reshape(64, 128), q, g, k, v)

time: 120 us -> 119 us (level)
  no operation moved by 1% of the time
where the time goes in v4:
time: 119 us; the launch traced here: 118 us
  Pallas kernels  111 us (93%)
  local copies, waits for them, and re-layouts  5.98 us (5%)
    pallas_call x1, Pallas kernels, gather(): pl.pallas_call(gather_kernel, out_shape=(jax.ShapeDtypeStruct((ROUNDS, 2,...  46.6 us
    pallas_call x1, Pallas kernels, reduce(): pl.pallas_call(reduce_kernel, out_shape=(jax.ShapeDtypeStruct((20, 2, 64,...  35.7 us
    pallas_call x1, Pallas kernels, attn(): pl.pallas_call(attn_kernel, out_shape=(jax.ShapeDtypeStruct((ROUNDS, 256,...  29 us
    transpose x1, local copies, waits for them, and re-layouts, per_device(): gh = jnp.transpose(grad_out, (2, 0, 1, 3))  2.48 us

profile of v4, /device:TPU:1, one launch (start us, length us, event | category | flops | bytes accessed | tf_op | source)
XLA Modules:
  0.0 117.9 jit_solution(325036823799280306)
XLA Ops:
  0.6 2.5 %copy_bitcast_fusion = (bf16[20,2,64,128]{3,2,1,0:T(8,128)(2,1)}, bf16[20,2,64,128]{3,2,1,0:T(8,128)(2,1)}) fusion(bf16[2,64,20,128]{3,1,2,0:T(8,128)(2,1)} %param.6, bf16[2,64,20,128]{3,1,2,0:T(8,128)(2,1)} %param.5), kind=kLoop, calls=%fused_computation | loop fusion | bytes 2621440 | tf_op jit(solution)/shard_map/transpose | solution.py:580
  3.1 46.6 %gather_units.1 = (bf16[10,2,128,128]{3,2,1,0:T(8,128)(2,1)}, bf16[10,2,128,128]{3,2,1,0:T(8,128)(2,1)}, bf16[32,256,128]{2,1,0:T(8,128)(2,1)}, bf16[32,256,128]{2,1,0:T(8,128)(2,1)}) custom-call(bf16[20,2,64,128]{3,2,1,0:T(8,128)(2,1)} %get-tuple-element.25.qh, bf16[20,2,64,128]{3,2,1,0:T(8,128)(2,1)} %get-tuple-element.24.gh, bf16[256,128]{1,0:T(8,128)(2,1)} %bitcast.26, ...), custom_call_target="tpu_custom_call" | custom-call | tf_op jit(solution)/shard_map/gather_units/pallas_call | solution.py:213
  49.7 29.0 %attn_grads.1 = (bf16[10,256,128]{2,1,0:T(8,128)(2,1)}, bf16[2,8192,128]{2,1,0:T(8,128)(2,1)}) custom-call(s32[8192]{0:T(1024)} %doc_s.1, s32[64,128]{1,0:T(8,128)} %bitcast.25, bf16[10,256,128]{2,1,0:T(8,128)(2,1)} %bitcast.23, bf16[10,256,128]{2,1,0:T(8,128)(2,1)} %bitcast.24, bf16[8192,128]{1,0:T(8,128)(2,1)} %bitcast.19, bf16[8192,128]{1,0:T(8,128)(2,1)} %bitcast.20), custom_call_target="tpu_custom_call" | custom-call | tf_op jit(solution)/shard_map/attn_grads/pallas_call | solution.py:396
  78.7 35.7 %reduce_grads.1 = (bf16[20,2,64,128]{3,2,1,0:T(8,128)(2,1)}, bf16[2,256,128]{2,1,0:T(8,128)(2,1)}) custom-call(bf16[10,2,128,128]{3,2,1,0:T(8,128)(2,1)} %bitcast.21, bf16[2,4,4,512,128]{4,3,2,1,0:T(8,128)(2,1)} %bitcast.18), custom_call_target="tpu_custom_call" | custom-call | tf_op jit(solution)/shard_map/reduce_grads/pallas_call | solution.py:559
  114.4 2.0 %copy.10 = bf16[2,64,20,128]{3,1,2,0:T(8,128)(2,1)} copy(bf16[2,64,20,128]{3,1,0,2:T(8,128)(2,1)} %bitcast.22) | data formatting | bytes 1310720
  116.4 1.5 %slice_bitcast_fusion = (bf16[256,1,128]{2,0,1:T(8,128)(2,1)}, bf16[256,1,128]{2,0,1:T(8,128)(2,1)}) fusion(bf16[2,256,128]{2,1,0:T(8,128)(2,1)} %get-tuple-element.18), kind=kLoop, calls=%fused_computation.2 | loop fusion | bytes 262144 | tf_op jit(solution)/shard_map/reshape;squeeze | solution.py:591

commit v5 on v4

--- a/solution.py
+++ b/solution.py
@@ -425,7 +425,8 @@
         return at_dev(seq_of(jnp.where(first_x, a, b), jnp.where(first_x, b, a), c), z)
 
     units = []
-    for r in range(ROUNDS):
+    for step in range(ROUNDS):
+        r = lax.rem(s + step, ROUNDS)
         n = unit_at(r, s)
         b = n // 5
         for hf in range(2):

time: 119 us -> 121 us (1.017)
  Pallas kernels: 111 us -> 114 us
    pallas_call x1, Pallas kernels: 35.7 us -> 37.1 us  [reduce(): pl.pallas_call(reduce_kernel, out_shape=(jax.ShapeDtypeStruct((20, 2, 64,...]
where the time goes in v5:
time: 121 us; the launch traced here: 120 us
  Pallas kernels  114 us (94%)
  local copies, waits for them, and re-layouts  5.98 us (5%)
    pallas_call x1, Pallas kernels, gather(): pl.pallas_call(gather_kernel, out_shape=(jax.ShapeDtypeStruct((ROUNDS, 2,...  46.6 us
    pallas_call x1, Pallas kernels, reduce(): pl.pallas_call(reduce_kernel, out_shape=(jax.ShapeDtypeStruct((20, 2, 64,...  37.1 us
    pallas_call x1, Pallas kernels, attn(): pl.pallas_call(attn_kernel, out_shape=(jax.ShapeDtypeStruct((ROUNDS, 256,...  29.8 us
    transpose x1, local copies, waits for them, and re-layouts, per_device(): gh = jnp.transpose(grad_out, (2, 0, 1, 3))  2.48 us

profile of v5, /device:TPU:1, one launch (start us, length us, event | category | flops | bytes accessed | tf_op | source)
XLA Modules:
  0.0 120.1 jit_solution(17211460785369142538)
XLA Ops:
  0.6 2.5 %copy_bitcast_fusion = (bf16[20,2,64,128]{3,2,1,0:T(8,128)(2,1)}, bf16[20,2,64,128]{3,2,1,0:T(8,128)(2,1)}) fusion(bf16[2,64,20,128]{3,1,2,0:T(8,128)(2,1)} %param.6, bf16[2,64,20,128]{3,1,2,0:T(8,128)(2,1)} %param.5), kind=kLoop, calls=%fused_computation | loop fusion | bytes 2621440 | tf_op jit(solution)/shard_map/transpose | solution.py:581
  3.1 46.6 %gather_units.1 = (bf16[10,2,128,128]{3,2,1,0:T(8,128)(2,1)}, bf16[10,2,128,128]{3,2,1,0:T(8,128)(2,1)}, bf16[32,256,128]{2,1,0:T(8,128)(2,1)}, bf16[32,256,128]{2,1,0:T(8,128)(2,1)}) custom-call(bf16[20,2,64,128]{3,2,1,0:T(8,128)(2,1)} %get-tuple-element.25.qh, bf16[20,2,64,128]{3,2,1,0:T(8,128)(2,1)} %get-tuple-element.24.gh, bf16[256,128]{1,0:T(8,128)(2,1)} %bitcast.26, ...), custom_call_target="tpu_custom_call" | custom-call | tf_op jit(solution)/shard_map/gather_units/pallas_call | solution.py:213
  49.7 29.8 %attn_grads.1 = (bf16[10,256,128]{2,1,0:T(8,128)(2,1)}, bf16[2,8192,128]{2,1,0:T(8,128)(2,1)}) custom-call(s32[8192]{0:T(1024)} %doc_s.1, s32[64,128]{1,0:T(8,128)} %bitcast.25, bf16[10,256,128]{2,1,0:T(8,128)(2,1)} %bitcast.23, bf16[10,256,128]{2,1,0:T(8,128)(2,1)} %bitcast.24, bf16[8192,128]{1,0:T(8,128)(2,1)} %bitcast.19, bf16[8192,128]{1,0:T(8,128)(2,1)} %bitcast.20), custom_call_target="tpu_custom_call" | custom-call | tf_op jit(solution)/shard_map/attn_grads/pallas_call | solution.py:396
  79.5 37.1 %reduce_grads.1 = (bf16[20,2,64,128]{3,2,1,0:T(8,128)(2,1)}, bf16[2,256,128]{2,1,0:T(8,128)(2,1)}) custom-call(bf16[10,2,128,128]{3,2,1,0:T(8,128)(2,1)} %bitcast.21, bf16[2,4,4,512,128]{4,3,2,1,0:T(8,128)(2,1)} %bitcast.18), custom_call_target="tpu_custom_call" | custom-call | tf_op jit(solution)/shard_map/reduce_grads/pallas_call | solution.py:560
  116.6 2.0 %copy.10 = bf16[2,64,20,128]{3,1,2,0:T(8,128)(2,1)} copy(bf16[2,64,20,128]{3,1,0,2:T(8,128)(2,1)} %bitcast.22) | data formatting | bytes 1310720
  118.6 1.5 %slice_bitcast_fusion = (bf16[256,1,128]{2,0,1:T(8,128)(2,1)}, bf16[256,1,128]{2,0,1:T(8,128)(2,1)}) fusion(bf16[2,256,128]{2,1,0:T(8,128)(2,1)} %get-tuple-element.18), kind=kLoop, calls=%fused_computation.2 | loop fusion | bytes 262144 | tf_op jit(solution)/shard_map/reshape;squeeze | solution.py:592
